TPU v7x, 512 devices: a whole 4x4x16 slice. The times are simulated.
512 devices in a mesh: dp: 32 (over y_lo, z), ctx: 16 (over y_hi, x, core).
Axes of the slice: x: 4, y: 4 (y_hi: 2, y_lo: 2; y = y_hi * 2 + y_lo), z: 16, core: 2. Of those that a mesh axis runs over, the one named last changes fastest.
Arguments:
- hidden_in: bfloat16 [32, 2048, 5376], P('dp', 'ctx'), may hold values from -30 to 30
- w_qkv: bfloat16 [5376, 512], P('ctx'), may hold values from -1 to 1
- d_attn: bfloat16 [32, 2048, 256], P('dp', 'ctx'), may hold values from -6 to 6
- range_len: int32 [32, 16], P('dp', 'ctx'), may hold values from 96 to 128, as said below
- doc_ids: int32 [32, 2048], P('dp', 'ctx'), may hold values from 0 to 1, never falling along the last dimension, each value on 1 to 1536 neighbouring positions
Outputs:
- d_x: bfloat16 [32, 2048, 5376], P('dp', 'ctx')
- d_w: float32 [5376, 512], P('ctx')
Inputs may be any that keep to these rules, and one draw needn't show every extreme that they name: `range_len`: every range holds between 96 and 128 live tokens; in every sequence one range holds exactly 128 and another exactly 96.
All inputs are finite; a program needn't handle non-finite values.
Results may differ from a plain program's by a relative error of at most 0.015.
Values may be sent and summed in bfloat16 or wider, within the bound.
A program may use at most 64 MiB of HBM per device.

v0:
```python
import jax
import jax.numpy as jnp
from jax import lax
from jax.sharding import PartitionSpec as P

HD = 128
WINDOW = 1024
QHEADS = 2
REACH = 11


score_scale = 168.0 ** (-0.5)
neg_fill = -1e30


def carried_in(value, axis, join, neutral):
    count, mine = (lax.axis_size(axis), lax.axis_index(axis))
    pieces = lax.all_gather(value, axis)
    subtotal = jnp.full_like(value, 0) + jnp.asarray(neutral, value.dtype)

    def hop(position, subtotal):
        longer = join(subtotal, pieces[position])
        return jnp.where(position < mine, longer, subtotal)

    return lax.fori_loop(0, count - 1, hop, subtotal)


def passed_along(value, axis, steps):
    count = lax.axis_size(axis)
    first, last = (max(0, -steps), min(count, count - steps))
    return lax.ppermute(value, axis, [(source, source + steps) for source in range(first, last)])


def rotary_tables(positions, head_size):
    half = head_size // 2
    freqs = 10000.0 ** (-(jnp.arange(half, dtype=jnp.float32) * 2.0) / head_size)
    angles = positions.astype(jnp.float32)[:, None] * freqs[None, :]
    return (jnp.cos(angles), jnp.sin(angles))


def rotate(values, cosine, sine, sign):
    half = values.shape[-1] // 2
    first = values[..., :half]
    second = values[..., half:]
    return jnp.concatenate(
        [first * cosine - sign * second * sine, second * cosine + sign * first * sine], axis=-1
    )


def allowed_pairs(query_meta, key_meta):
    qpos = query_meta[:, 0][:, None]
    kpos = key_meta[:, 0][None, :]
    same_doc = query_meta[:, 1][:, None] == key_meta[:, 1][None, :]
    both_live = (query_meta[:, 2][:, None] == 1) & (key_meta[:, 2][None, :] == 1)
    return both_live & same_doc & (kpos <= qpos) & (qpos - kpos < WINDOW)


def add_ints(earlier, later):
    return earlier + later


def body(hidden_in, w_qkv, d_attn, range_len, doc_ids):
    tokens = hidden_in[0]
    cap = tokens.shape[0]
    groups = lax.axis_size("ctx")
    own_len = range_len[0, 0]
    start = carried_in(own_len, "ctx", add_ints, jnp.int32(0))
    slot = jnp.arange(cap, dtype=jnp.int32)
    live = slot < own_len
    meta = jnp.stack([start + slot, doc_ids[0], live.astype(jnp.int32)], axis=1)
    cosine, sine = rotary_tables(meta[:, 0], HD)
    nq = QHEADS * HD
    x_cols = lax.all_to_all(tokens, "ctx", split_axis=1, concat_axis=0, tiled=True)
    proj = jnp.dot(
        tokens, lax.all_gather(w_qkv, "ctx", axis=0, tiled=True), preferred_element_type=jnp.float32
    )
    queries = rotate(
        proj[:, :nq].reshape(cap, QHEADS, HD), cosine[:, None, :], sine[:, None, :], 1.0
    ).astype(jnp.bfloat16)
    keys = rotate(proj[:, nq : nq + HD], cosine, sine, 1.0).astype(jnp.bfloat16)
    values = proj[:, nq + HD :].astype(jnp.bfloat16)
    key_pack = jnp.concatenate([keys, values], axis=1)
    grad_out = d_attn[0].reshape(cap, QHEADS, HD)
    top = jnp.full((QHEADS, cap), neg_fill, jnp.float32)
    pack = lax.all_gather(key_pack, "ctx", axis=0, tiled=True)
    key_meta = lax.all_gather(meta, "ctx", axis=0, tiled=True)
    scores = score_scale * jnp.einsum(
        "qhd,kd->hqk", queries, pack[:, :HD], preferred_element_type=jnp.float32
    )
    dots = jnp.einsum("qhd,kd->hqk", grad_out, pack[:, HD:], preferred_element_type=jnp.float32)
    allowed = allowed_pairs(meta, key_meta)[None]
    new_top = jnp.maximum(top, jnp.max(jnp.where(allowed, scores, neg_fill), axis=2))
    expo = jnp.where(allowed, jnp.exp(scores - new_top[:, :, None]), 0.0)
    carry = (new_top, jnp.sum(expo, axis=2), jnp.sum(expo * dots, axis=2))
    top, total, weighted = carry
    live_rows = live[None, :]
    safe_total = jnp.where(live_rows, total, 1.0)
    lse = jnp.where(live_rows, top + jnp.log(safe_total), 0.0)
    delta = jnp.where(live_rows, weighted / safe_total, 0.0)
    pack = lax.all_gather(key_pack, "ctx", axis=0, tiled=True)
    key_meta = lax.all_gather(meta, "ctx", axis=0, tiled=True)
    scores = score_scale * jnp.einsum(
        "qhd,kd->hqk", queries, pack[:, :HD], preferred_element_type=jnp.float32
    )
    dots = jnp.einsum("qhd,kd->hqk", grad_out, pack[:, HD:], preferred_element_type=jnp.float32)
    allowed = allowed_pairs(meta, key_meta)[None]
    probs = jnp.where(allowed, jnp.exp(scores - lse[:, :, None]), 0.0)
    mixed = (probs * (dots - delta[:, :, None])).astype(jnp.bfloat16)
    dq_sum = jnp.einsum("hqk,kd->qhd", mixed, pack[:, :HD], preferred_element_type=jnp.float32)
    dq = score_scale * dq_sum

    def key_step(carry, piece):
        dkey, dval = carry
        query_pack, stats, query_meta = piece
        rows = query_pack.shape[0]
        query_b = query_pack[:, :nq].reshape(rows, QHEADS, HD)
        grad_b = query_pack[:, nq:].reshape(rows, QHEADS, HD)
        scores = score_scale * jnp.einsum(
            "qhd,kd->hqk", query_b, keys, preferred_element_type=jnp.float32
        )
        dots = jnp.einsum("qhd,kd->hqk", grad_b, values, preferred_element_type=jnp.float32)
        allowed = allowed_pairs(query_meta, meta)[None]
        lse_b = stats[:, :QHEADS].T
        delta_b = stats[:, QHEADS:].T
        probs = jnp.where(allowed, jnp.exp(scores - lse_b[:, :, None]), 0.0)
        mixed = (probs * (dots - delta_b[:, :, None])).astype(jnp.bfloat16)
        dval = dval + jnp.einsum(
            "hqk,qhd->kd", probs.astype(jnp.bfloat16), grad_b, preferred_element_type=jnp.float32
        )
        dkey = dkey + jnp.einsum("hqk,qhd->kd", mixed, query_b, preferred_element_type=jnp.float32)
        return (dkey, dval)

    query_pack = jnp.concatenate([queries.reshape(cap, nq), d_attn[0]], axis=1)
    stats = jnp.concatenate([lse.T, delta.T], axis=1)
    init_keys = (jnp.zeros((cap, HD), jnp.float32), jnp.zeros((cap, HD), jnp.float32))
    carry = key_step(init_keys, (query_pack, stats, meta))
    for hop in range(1, min(REACH, groups - 1) + 1):
        later = (
            passed_along(query_pack.astype(jnp.float32), "ctx", -hop).astype(query_pack.dtype),
            passed_along(stats, "ctx", -hop),
            passed_along(meta, "ctx", -hop),
        )
        carry = key_step(carry, later)
    dkey, dval = carry
    dq_pre = rotate(dq, cosine[:, None, :], sine[:, None, :], -1.0).reshape(cap, nq)
    dk_pre = rotate(score_scale * dkey, cosine, sine, -1.0)
    d_proj = jnp.concatenate([dq_pre, dk_pre, dval], axis=1).astype(jnp.bfloat16)
    every = lax.all_gather(d_proj, "ctx", axis=0, tiled=True)
    partial_w = lax.dot_general(
        x_cols, every, (((0,), (0,)), ((), ())), preferred_element_type=jnp.float32
    )
    d_w = lax.psum(partial_w, "dp")
    rows_back = lax.dot_general(
        every, w_qkv, (((1,), (1,)), ((), ())), preferred_element_type=jnp.float32
    ).astype(jnp.bfloat16)
    d_x = lax.all_to_all(rows_back, "ctx", split_axis=0, concat_axis=1, tiled=True)
    return (d_x[None], d_w)


def solution(mesh):
    return jax.shard_map(
        body,
        mesh=mesh,
        in_specs=(
            P("dp", "ctx", None),
            P("ctx", None),
            P("dp", "ctx", None),
            P("dp", "ctx"),
            P("dp", "ctx"),
        ),
        out_specs=(P("dp", "ctx", None), P("ctx", None)),
        check_vma=False,
    )
```

profile of v0, /device:TPU:2, one launch (start us, length us, event | category | flops | bytes accessed | tf_op | source)
XLA Modules:
  0.0 598.6 jit_solution(13358182207900474301)
XLA Ops:
  10.6 12.8 %all-reduce = s32[16]{0:T(128)S(1)} all-reduce(s32[16]{0:T(128)S(1)} %bitcast_dynamic-update-slice_fusion), channel_id=2, replica_groups=mesh['dp'=32,'ctx'=16] {'ctx'}, use_global_device_ids=true, to_apply=%add | all-reduce | flops 16 | bytes 128 | tf_op jit(solution)/shard_map/all_gather | solution.py:18
  23.4 20.2 %while.13 = (s32[]{:T(128)}, s32[]{:T(128)}, s32[]{:T(128)}, s32[16]{0:T(128)S(1)}, s32[]{:T(128)}) while((s32[]{:T(128)}, s32[]{:T(128)}, s32[]{:T(128)}, s32[16]{0:T(128)S(1)}, s32[]{:T(128)}) %tuple.92), condition=%wide.region_1.2_spmd, body=%wide.region_0.1_spmd.sunk | while | flops 5 | bytes 107 | solution.py:25
  44.4 1.9 collective-permute-start
  46.3 3.1 collective-permute-start.3
  53.2 23.6 %all_gather.20 = s32[2048,3]{0,1:T(4,128)S(1)} all-gather(s32[128,3]{0,1:T(4,128)S(1)} %pad_add_fusion), channel_id=1, replica_groups=mesh['dp'=32,'ctx'=16] {'ctx'}, dimensions={0}, use_global_device_ids=true | all-gather | bytes 26112 | tf_op jit(solution)/shard_map/all_gather | solution.py:101
  76.9 2.4 fusion.122
  87.4 10.6 %collective-permute-done.30 = s32[128,3]{0,1:T(4,128)S(1)} collective-permute-done((s32[128,3]{0,1:T(4,128)S(1)}, s32[128,3]{0,1:T(4,128)S(1)}, u32[]{:S(2)}, u32[]{:S(2)}) %collective-permute-start.30) | collective-permute-done | bytes 1568 | tf_op jit(solution)/shard_map/ppermute | solution.py:31
  99.4 6.5 %collective-permute-done.15 = s32[128,3]{0,1:T(4,128)S(1)} collective-permute-done((s32[128,3]{0,1:T(4,128)S(1)}, s32[128,3]{0,1:T(4,128)S(1)}, u32[]{:S(2)}, u32[]{:S(2)}) %collective-permute-start.15) | collective-permute-done | bytes 1568 | tf_op jit(solution)/shard_map/ppermute | solution.py:31
  107.5 1.6 fusion.149
  109.1 3.9 fusion.6
  114.3 1.9 collective-permute-start.4
  132.5 4.2 collective-permute-done.16
  138.6 1.9 collective-permute-start.1
  140.6 9.5 %collective-permute-done.22 = bf16[128,512]{0,1:T(8,128)(2,1)S(1)} collective-permute-done((bf16[128,512]{0,1:T(8,128)(2,1)S(1)}, bf16[128,512]{0,1:T(8,128)(2,1)S(1)}, u32[]{:S(2)}, u32[]{:S(2)}) %collective-permute-start.22) | collective-permute-done | bytes 131104 | tf_op jit(solution)/shard_map/ppermute | solution.py:31
  150.8 42.6 %all-gather.7.cloned.1.call-done = bf16[2048,256]{1,0:T(8,128)(2,1)} async-done(((bf16[128,256]{1,0:T(8,128)(2,1)}), bf16[2048,256]{1,0:T(8,128)(2,1)}) %all-gather.7.cloned.1.call-update) | async-done | bytes 1048592 | tf_op jit(solution)/shard_map/all_gather | solution.py:100
  193.4 1.6 select_reduce_fusion
  195.1 1.9 fusion.1
  198.2 2.7 collective-permute-start.5
  206.9 1.9 convolution_bitcast_fusion.36
  208.8 1.7 convolution_bitcast_fusion.24
  210.5 2.5 fusion.11
  217.8 1.6 convolution_bitcast_fusion.22
  234.6 1.9 collective-permute-start.2
  241.2 2.6 collective-permute-done.32
  249.4 11.0 %all-to-all-start.1 = ((bf16[128,16,336]{0,2,1:T(8,128)(2,1)}), bf16[128,16,336]{0,2,1:T(8,128)(2,1)S(1)}, u32[]{:S(2)}, u32[]{:S(2)}) async-start(bf16[128,16,336]{0,2,1:T(8,128)(2,1)} %bitcast.160), calls=%async_computation.1 | async-start | bytes 2752512 | tf_op jit(solution)/shard_map/all_to_all | solution.py:73
  260.4 58.4 %all-gather.9.cloned.1.call-done = bf16[2048,512]{0,1:T(8,128)(2,1)} async-done(((bf16[128,512]{0,1:T(8,128)(2,1)}), bf16[2048,512]{0,1:T(8,128)(2,1)}) %all-gather.9.cloned.1.call-update) | async-done | bytes 2097168 | tf_op jit(solution)/shard_map/all_gather | solution.py:148
  318.7 2.5 fusion.2
  322.5 4.5 all-to-all-start
  327.1 3.4 fusion.8
  330.5 15.0 %all-to-all-done = bf16[16,128,336]{1,2,0:T(8,128)(2,1)S(1)} async-done(((bf16[16,128,336]{1,2,0:T(8,128)(2,1)}), bf16[16,128,336]{1,2,0:T(8,128)(2,1)S(1)}, u32[]{:S(2)}, u32[]{:S(2)}) %all-to-all-start) | async-done | bytes 1376288 | tf_op jit(solution)/shard_map/all_to_all | solution.py:156
  347.0 243.1 %all-reduce.3.cloned.1.call-done = f32[336,512]{1,0:T(8,128)} async-done(((f32[336,512]{1,0:T(8,128)}), f32[336,512]{1,0:T(8,128)}) %all-reduce.3.cloned.1.call-update) | async-done | bytes 688144 | tf_op jit(solution)/shard_map/psum | solution.py:152
  590.0 2.0 copy.406
  (272 shorter events, 87.8 us)
Async XLA Ops:
  7.2 102.0 %all-gather.5.cloned.1.call-start = ((), (), s32[]{:S(2)}) async-start(), calls=%async_computation.2 | async-start | bytes 5849088 | tf_op jit(solution)/shard_map/all_gather | solution.py:75
  7.9 185.5 %all-gather.7.cloned.1.call-start = ((), (), s32[]{:S(2)}) async-start(), calls=%async_computation.3 | async-start | bytes 1114112 | tf_op jit(solution)/shard_map/all_gather | solution.py:100
  44.4 36.4 %collective-permute-start = (s32[128,3]{0,1:T(4,128)S(1)}, s32[128,3]{0,1:T(4,128)S(1)}, u32[]{:S(2)}, u32[]{:S(2)}) collective-permute-start(s32[128,3]{0,1:T(4,128)S(1)} %pad_add_fusion), channel_id=1, source_target_pairs={{1,0},{2,1},{3,2},{4,3},{5,4},{6,5},{7,6},{8,7},{9,8},{10,9},{11,1... | collective-permute-start | bytes 4616 | tf_op jit(solution)/shard_map/ppermute | solution.py:31
  46.3 39.8 %collective-permute-start.3 = (s32[128,3]{0,1:T(4,128)S(1)}, s32[128,3]{0,1:T(4,128)S(1)}, u32[]{:S(2)}, u32[]{:S(2)}) collective-permute-start(s32[128,3]{0,1:T(4,128)S(1)} %pad_add_fusion), channel_id=1, source_target_pairs={{2,0},{3,1},{4,2},{5,3},{6,4},{7,5},{8,6},{9,7},{10,8},{11,9},{12,... | collective-permute-start | bytes 4616 | tf_op jit(solution)/shard_map/ppermute | solution.py:31
  49.3 35.4 %collective-permute-start.6 = (s32[128,3]{0,1:T(4,128)S(1)}, s32[128,3]{0,1:T(4,128)S(1)}, u32[]{:S(2)}, u32[]{:S(2)}) collective-permute-start(s32[128,3]{0,1:T(4,128)S(1)} %pad_add_fusion), channel_id=1, source_target_pairs={{3,0},{4,1},{5,2},{6,3},{7,4},{8,5},{9,6},{10,7},{11,8},{12,9},{13... | collective-permute-start | bytes 4616 | tf_op jit(solution)/shard_map/ppermute | solution.py:31
  50.6 32.8 %collective-permute-start.18 = (s32[128,3]{0,1:T(4,128)S(1)}, s32[128,3]{0,1:T(4,128)S(1)}, u32[]{:S(2)}, u32[]{:S(2)}) collective-permute-start(s32[128,3]{0,1:T(4,128)S(1)} %pad_add_fusion), channel_id=1, source_target_pairs={{7,0},{8,1},{9,2},{10,3},{11,4},{12,5},{13,6},{14,7},{15,8},{23,16... | collective-permute-start | bytes 4616 | tf_op jit(solution)/shard_map/ppermute | solution.py:31
  51.9 30.2 %collective-permute-start.24 = (s32[128,3]{0,1:T(4,128)S(1)}, s32[128,3]{0,1:T(4,128)S(1)}, u32[]{:S(2)}, u32[]{:S(2)}) collective-permute-start(s32[128,3]{0,1:T(4,128)S(1)} %pad_add_fusion), channel_id=1, source_target_pairs={{9,0},{10,1},{11,2},{12,3},{13,4},{14,5},{15,6},{25,16},{26,17},{2... | collective-permute-start | bytes 4616 | tf_op jit(solution)/shard_map/ppermute | solution.py:31
  80.8 18.6 %collective-permute-start.9 = (s32[128,3]{0,1:T(4,128)S(1)}, s32[128,3]{0,1:T(4,128)S(1)}, u32[]{:S(2)}, u32[]{:S(2)}) collective-permute-start(s32[128,3]{0,1:T(4,128)S(1)} %pad_add_fusion), channel_id=1, source_target_pairs={{4,0},{5,1},{6,2},{7,3},{8,4},{9,5},{10,6},{11,7},{12,8},{13,9},{1... | collective-permute-start | bytes 4616 | tf_op jit(solution)/shard_map/ppermute | solution.py:31
  82.1 17.3 %collective-permute-start.12 = (s32[128,3]{0,1:T(4,128)S(1)}, s32[128,3]{0,1:T(4,128)S(1)}, u32[]{:S(2)}, u32[]{:S(2)}) collective-permute-start(s32[128,3]{0,1:T(4,128)S(1)} %pad_add_fusion), channel_id=1, source_target_pairs={{5,0},{6,1},{7,2},{8,3},{9,4},{10,5},{11,6},{12,7},{13,8},{14,9},{... | collective-permute-start | bytes 4616 | tf_op jit(solution)/shard_map/ppermute | solution.py:31
  83.4 15.9 %collective-permute-start.21 = (s32[128,3]{0,1:T(4,128)S(1)}, s32[128,3]{0,1:T(4,128)S(1)}, u32[]{:S(2)}, u32[]{:S(2)}) collective-permute-start(s32[128,3]{0,1:T(4,128)S(1)} %pad_add_fusion), channel_id=1, source_target_pairs={{8,0},{9,1},{10,2},{11,3},{12,4},{13,5},{14,6},{15,7},{24,16},{25,... | collective-permute-start | bytes 4616 | tf_op jit(solution)/shard_map/ppermute | solution.py:31
  84.7 14.6 %collective-permute-start.27 = (s32[128,3]{0,1:T(4,128)S(1)}, s32[128,3]{0,1:T(4,128)S(1)}, u32[]{:S(2)}, u32[]{:S(2)}) collective-permute-start(s32[128,3]{0,1:T(4,128)S(1)} %pad_add_fusion), channel_id=1, source_target_pairs={{10,0},{11,1},{12,2},{13,3},{14,4},{15,5},{26,16},{27,17},{28,18},... | collective-permute-start | bytes 4616 | tf_op jit(solution)/shard_map/ppermute | solution.py:31
  86.1 11.9 %collective-permute-start.30 = (s32[128,3]{0,1:T(4,128)S(1)}, s32[128,3]{0,1:T(4,128)S(1)}, u32[]{:S(2)}, u32[]{:S(2)}) collective-permute-start(s32[128,3]{0,1:T(4,128)S(1)} %pad_add_fusion), channel_id=1, source_target_pairs={{11,0},{12,1},{13,2},{14,3},{15,4},{27,16},{28,17},{29,18},{30,19}... | collective-permute-start | bytes 4616 | tf_op jit(solution)/shard_map/ppermute | solution.py:31
  120.3 16.4 %collective-permute-start.16 = (bf16[128,512]{0,1:T(8,128)(2,1)S(1)}, bf16[128,512]{0,1:T(8,128)(2,1)S(1)}, u32[]{:S(2)}, u32[]{:S(2)}) collective-permute-start(bf16[128,512]{0,1:T(8,128)(2,1)S(1)} %maximum_convert_fusion.1), channel_id=1, source_target_pairs={{6,0},{7,1},{8,2},{9,3},{10,4},{11,5},{12,6},{13,7},{14,8},{15,9},... | collective-permute-start | bytes 393224 | tf_op jit(solution)/shard_map/ppermute | solution.py:31
  122.6 196.1 %all-gather.9.cloned.1.call-start = ((), (), s32[]{:S(2)}) async-start(), calls=%async_computation.4 | async-start | bytes 2228224 | tf_op jit(solution)/shard_map/all_gather | solution.py:148
  123.4 15.3 %collective-permute-start.19 = (bf16[128,512]{0,1:T(8,128)(2,1)S(1)}, bf16[128,512]{0,1:T(8,128)(2,1)S(1)}, u32[]{:S(2)}, u32[]{:S(2)}) collective-permute-start(bf16[128,512]{0,1:T(8,128)(2,1)S(1)} %maximum_convert_fusion.1), channel_id=1, source_target_pairs={{7,0},{8,1},{9,2},{10,3},{11,4},{12,5},{13,6},{14,7},{15,8},{23,16... | collective-permute-start | bytes 393224 | tf_op jit(solution)/shard_map/ppermute | solution.py:31
  125.3 24.7 %collective-permute-start.22 = (bf16[128,512]{0,1:T(8,128)(2,1)S(1)}, bf16[128,512]{0,1:T(8,128)(2,1)S(1)}, u32[]{:S(2)}, u32[]{:S(2)}) collective-permute-start(bf16[128,512]{0,1:T(8,128)(2,1)S(1)} %maximum_convert_fusion.1), channel_id=1, source_target_pairs={{8,0},{9,1},{10,2},{11,3},{12,4},{13,5},{14,6},{15,7},{24,16},{25,... | collective-permute-start | bytes 393224 | tf_op jit(solution)/shard_map/ppermute | solution.py:31
  128.6 21.5 %collective-permute-start.25 = (bf16[128,512]{0,1:T(8,128)(2,1)S(1)}, bf16[128,512]{0,1:T(8,128)(2,1)S(1)}, u32[]{:S(2)}, u32[]{:S(2)}) collective-permute-start(bf16[128,512]{0,1:T(8,128)(2,1)S(1)} %maximum_convert_fusion.1), channel_id=1, source_target_pairs={{9,0},{10,1},{11,2},{12,3},{13,4},{14,5},{15,6},{25,16},{26,17},{2... | collective-permute-start | bytes 393224 | tf_op jit(solution)/shard_map/ppermute | solution.py:31
  130.6 19.6 %collective-permute-start.28 = (bf16[128,512]{0,1:T(8,128)(2,1)S(1)}, bf16[128,512]{0,1:T(8,128)(2,1)S(1)}, u32[]{:S(2)}, u32[]{:S(2)}) collective-permute-start(bf16[128,512]{0,1:T(8,128)(2,1)S(1)} %maximum_convert_fusion.1), channel_id=1, source_target_pairs={{10,0},{11,1},{12,2},{13,3},{14,4},{15,5},{26,16},{27,17},{28,18},... | collective-permute-start | bytes 393224 | tf_op jit(solution)/shard_map/ppermute | solution.py:31
  136.7 13.5 %collective-permute-start.31 = (bf16[128,512]{0,1:T(8,128)(2,1)S(1)}, bf16[128,512]{0,1:T(8,128)(2,1)S(1)}, u32[]{:S(2)}, u32[]{:S(2)}) collective-permute-start(bf16[128,512]{0,1:T(8,128)(2,1)S(1)} %maximum_convert_fusion.1), channel_id=1, source_target_pairs={{11,0},{12,1},{13,2},{14,3},{15,4},{27,16},{28,17},{29,18},{30,19}... | collective-permute-start | bytes 393224 | tf_op jit(solution)/shard_map/ppermute | solution.py:31
  198.2 15.3 %collective-permute-start.5 = (f32[128,4]{0,1:T(4,128)}, f32[128,4]{0,1:T(4,128)}, u32[]{:S(2)}, u32[]{:S(2)}) collective-permute-start(f32[128,4]{0,1:T(4,128)} %pad_maximum_fusion.3), channel_id=1, source_target_pairs={{2,0},{3,1},{4,2},{5,3},{6,4},{7,5},{8,6},{9,7},{10,8},{11,9},{12,... | collective-permute-start | bytes 6152 | tf_op jit(solution)/shard_map/ppermute | solution.py:31
  200.9 18.5 %collective-permute-start.8 = (f32[128,4]{0,1:T(4,128)}, f32[128,4]{0,1:T(4,128)}, u32[]{:S(2)}, u32[]{:S(2)}) collective-permute-start(f32[128,4]{0,1:T(4,128)} %pad_maximum_fusion.3), channel_id=1, source_target_pairs={{3,0},{4,1},{5,2},{6,3},{7,4},{8,5},{9,6},{10,7},{11,8},{12,9},{13... | collective-permute-start | bytes 6152 | tf_op jit(solution)/shard_map/ppermute | solution.py:31
  202.2 22.3 %collective-permute-start.11 = (f32[128,4]{0,1:T(4,128)}, f32[128,4]{0,1:T(4,128)}, u32[]{:S(2)}, u32[]{:S(2)}) collective-permute-start(f32[128,4]{0,1:T(4,128)} %pad_maximum_fusion.3), channel_id=1, source_target_pairs={{4,0},{5,1},{6,2},{7,3},{8,4},{9,5},{10,6},{11,7},{12,8},{13,9},{1... | collective-permute-start | bytes 6152 | tf_op jit(solution)/shard_map/ppermute | solution.py:31
  203.5 24.4 %collective-permute-start.14 = (f32[128,4]{0,1:T(4,128)}, f32[128,4]{0,1:T(4,128)}, u32[]{:S(2)}, u32[]{:S(2)}) collective-permute-start(f32[128,4]{0,1:T(4,128)} %pad_maximum_fusion.3), channel_id=1, source_target_pairs={{5,0},{6,1},{7,2},{8,3},{9,4},{10,5},{11,6},{12,7},{13,8},{14,9},{... | collective-permute-start | bytes 6152 | tf_op jit(solution)/shard_map/ppermute | solution.py:31
  204.8 26.5 %collective-permute-start.17 = (f32[128,4]{0,1:T(4,128)}, f32[128,4]{0,1:T(4,128)}, u32[]{:S(2)}, u32[]{:S(2)}) collective-permute-start(f32[128,4]{0,1:T(4,128)} %pad_maximum_fusion.3), channel_id=1, source_target_pairs={{6,0},{7,1},{8,2},{9,3},{10,4},{11,5},{12,6},{13,7},{14,8},{15,9},... | collective-permute-start | bytes 6152 | tf_op jit(solution)/shard_map/ppermute | solution.py:31
  213.5 21.1 %collective-permute-start.20 = (f32[128,4]{0,1:T(4,128)}, f32[128,4]{0,1:T(4,128)S(1)}, u32[]{:S(2)}, u32[]{:S(2)}) collective-permute-start(f32[128,4]{0,1:T(4,128)} %pad_maximum_fusion.3), channel_id=1, source_target_pairs={{7,0},{8,1},{9,2},{10,3},{11,4},{12,5},{13,6},{14,7},{15,8},{23,16... | collective-permute-start | bytes 6152 | tf_op jit(solution)/shard_map/ppermute | solution.py:31
  219.4 18.4 %collective-permute-start.23 = (f32[128,4]{0,1:T(4,128)}, f32[128,4]{0,1:T(4,128)S(1)}, u32[]{:S(2)}, u32[]{:S(2)}) collective-permute-start(f32[128,4]{0,1:T(4,128)} %pad_maximum_fusion.3), channel_id=1, source_target_pairs={{8,0},{9,1},{10,2},{11,3},{12,4},{13,5},{14,6},{15,7},{24,16},{25,... | collective-permute-start | bytes 6152 | tf_op jit(solution)/shard_map/ppermute | solution.py:31
  224.5 14.7 %collective-permute-start.26 = (f32[128,4]{0,1:T(4,128)}, f32[128,4]{0,1:T(4,128)S(1)}, u32[]{:S(2)}, u32[]{:S(2)}) collective-permute-start(f32[128,4]{0,1:T(4,128)} %pad_maximum_fusion.3), channel_id=1, source_target_pairs={{9,0},{10,1},{11,2},{12,3},{13,4},{14,5},{15,6},{25,16},{26,17},{2... | collective-permute-start | bytes 6152 | tf_op jit(solution)/shard_map/ppermute | solution.py:31
  227.9 12.7 %collective-permute-start.29 = (f32[128,4]{0,1:T(4,128)}, f32[128,4]{0,1:T(4,128)S(1)}, u32[]{:S(2)}, u32[]{:S(2)}) collective-permute-start(f32[128,4]{0,1:T(4,128)} %pad_maximum_fusion.3), channel_id=1, source_target_pairs={{10,0},{11,1},{12,2},{13,3},{14,4},{15,5},{26,16},{27,17},{28,18},... | collective-permute-start | bytes 6152 | tf_op jit(solution)/shard_map/ppermute | solution.py:31
  231.2 12.6 %collective-permute-start.32 = (f32[128,4]{0,1:T(4,128)}, f32[128,4]{0,1:T(4,128)S(1)}, u32[]{:S(2)}, u32[]{:S(2)}) collective-permute-start(f32[128,4]{0,1:T(4,128)} %pad_maximum_fusion.3), channel_id=1, source_target_pairs={{11,0},{12,1},{13,2},{14,3},{15,4},{27,16},{28,17},{29,18},{30,19}... | collective-permute-start | bytes 6152 | tf_op jit(solution)/shard_map/ppermute | solution.py:31
  249.4 73.1 %all-to-all-start.1 = ((bf16[128,16,336]{0,2,1:T(8,128)(2,1)}), bf16[128,16,336]{0,2,1:T(8,128)(2,1)S(1)}, u32[]{:S(2)}, u32[]{:S(2)}) async-start(bf16[128,16,336]{0,2,1:T(8,128)(2,1)} %bitcast.160), calls=%async_computation.1 | async-start | bytes 2752512 | tf_op jit(solution)/shard_map/all_to_all | solution.py:73
  322.5 22.9 %all-to-all-start = ((bf16[16,128,336]{1,2,0:T(8,128)(2,1)}), bf16[16,128,336]{1,2,0:T(8,128)(2,1)S(1)}, u32[]{:S(2)}, u32[]{:S(2)}) async-start(bf16[16,128,336]{1,2,0:T(8,128)(2,1)} %bitcast.632), calls=%async_computation | async-start | bytes 2752512 | tf_op jit(solution)/shard_map/all_to_all | solution.py:156
  327.0 263.0 %all-reduce.3.cloned.1.call-start = ((), (), s32[]{:S(2)}) async-start(), calls=%async_computation.5 | async-start | bytes 1376256 | tf_op jit(solution)/shard_map/psum | solution.py:152
  (42 other events, 555.0 us)
Sparse Core Ops, SparseCore 0:
  11.3 80.5 all-gather.4
  122.7 70.6 all-gather.6
  248.0 70.6 all-gather.8
  331.0 258.9 all-reduce.2
where the time goes:
time: 600 us; the launch traced here: 599 us
  waiting for transfers between devices  395 us (66%)
  starting transfers between devices  63.8 us (11%)
  matrix products  37 us (6%)
  blocking collectives  36.4 us (6%)
  local copies, waits for them, and re-layouts  30.3 us (5%)
  between operations  15.8 us (3%)
  loops' own time  10.5 us (2%)
  other arithmetic  9.7 us (2%)
    psum x1, waiting for transfers between devices, body(): d_w = lax.psum(partial_w, 'dp')  243 us
    all_gather x1, waiting for transfers between devices, body(): every = lax.all_gather(d_proj, 'ctx', axis=0, tiled=True)  58.4 us
    ppermute x33, starting transfers between devices, passed_along(): lax.ppermute(value, axis, [(source, source + steps) for source in range(f...  48.1 us
    all_gather x1, waiting for transfers between devices, body(): pack = lax.all_gather(key_pack, 'ctx', axis=0, tiled=True)  42.6 us
    ppermute x33, waiting for transfers between devices, passed_along(): lax.ppermute(value, axis, [(source, source + steps) for source in range(f...  35.4 us
    all_gather x1, blocking collectives, body(): key_meta = lax.all_gather(meta, 'ctx', axis=0, tiled=True)  23.6 us
    all_to_all x1, waiting for transfers between devices, body(): lax.all_to_all(rows_back, 'ctx', split_axis=0, concat_axis=1, tiled=True)  15 us
    all_gather x1, blocking collectives, carried_in(): pieces = lax.all_gather(value, axis)  12.8 us
  transfers between devices with their start and end apart: 39, of which 12 were waited for; matrix products, arithmetic and copies ran while one was open for 10% of the time, Pallas kernels for 0%

commit v1 on v0

v1 whole, which is shorter than its diff:
```python
import functools

import jax
import jax.numpy as jnp
import numpy as np
from jax import lax
from jax.experimental import pallas as pl
from jax.experimental.pallas import tpu as pltpu
from jax.sharding import PartitionSpec as P

HD = 128
WINDOW = 1024
CAP = 128
D = 5376
QKV = 512
RANGES = 16
CHIPS = 8
ROWS = D // RANGES
WIDE = D // CHIPS
REACH = 11
SLOTS = REACH + 1
DOC_STEP = 4096.0
FAR = 1.0e6
NEG = -1.0e30
SCALE = 168.0 ** (-0.5)
MESH = pl.DeviceIdType.MESH
F32 = jnp.float32
BF16 = jnp.bfloat16


def nt(a, b):
    return lax.dot_general(a, b, (((1,), (1,)), ((), ())), preferred_element_type=F32)


def tn(a, b):
    return lax.dot_general(a, b, (((0,), (0,)), ((), ())), preferred_element_type=F32)


def nn(a, b):
    return jnp.dot(a, b, preferred_element_type=F32)


def kernel(
    zn,
    x_ref, w_ref, g_ref, len_ref, doc_ref, freq_ref,
    dx_ref, dwt_ref,
    meta, keypos, xt, xall, wall, part, projr, acc, qt, qs, gs, gt, kvt, sbuf, dbuf, pbuf, dsbuf,
    dkvs, dkvr, dpt, dxs, dxt, a1s, a1r, tb, a2s, a2r, ub, a3s, a3r, ag,
    meta_s, meta_r, w_s, w_r, x_s, x_r, p_s, p_r, kv_s, kv_r, dk_s, dk_r, dp_s, dp_r, dx_s, dx_r,
    a1_s, a1_r, a2_s, a2_r, a3_s, a3_r, ag_s, ag_r, f_s, f_r,
):
    dp = lax.axis_index("dp")
    ctx = lax.axis_index("ctx")
    zi, yl = dp % zn, dp // zn
    chip, core = ctx // 2, ctx % 2
    rz = 256 // zn

    def at(d, c):
        return {"dp": d, "ctx": c}

    def remote(src, dst, ss, rs, dev):
        return pltpu.make_async_remote_copy(
            src_ref=src, dst_ref=dst, send_sem=ss, recv_sem=rs, device_id=dev, device_id_type=MESH
        )

    def lanes(i):
        return pl.ds(pl.multiple_of(i * 128, 128), 128)

    def chip_at(j):
        return at(dp, ((chip + j) % CHIPS) * 2 + core)

    sibling = at(dp, chip * 2 + (1 - core))
    ypair = at((1 - yl) * zn + zi, ctx)

    def zpeer(j):
        return at(yl * zn + (zi + j) % zn, ctx)

    barrier = pltpu.get_barrier_semaphore()

    def greet_ctx(j, carry):
        pl.semaphore_signal(barrier, inc=1, device_id=at(dp, (ctx + j) % RANGES), device_id_type=MESH)
        return carry

    def greet_z(j, carry):
        pl.semaphore_signal(barrier, inc=1, device_id=zpeer(j), device_id_type=MESH)
        return carry

    lax.fori_loop(1, RANGES, greet_ctx, 0)
    lax.fori_loop(1, zn, greet_z, 0)
    pl.semaphore_signal(barrier, inc=1, device_id=ypair, device_id_type=MESH)

    row = lax.broadcasted_iota(jnp.int32, (8, 128), 0)
    meta[ctx] = jnp.where(
        row == 0,
        jnp.broadcast_to(doc_ref[...], (8, 128)),
        jnp.broadcast_to(len_ref[...], (8, 128)),
    )
    for j in range(1, SLOTS):
        @pl.when(ctx - j < 0)
        def _():
            kvt[:, j * 128 : (j + 1) * 128] = jnp.zeros((256, 128), BF16)

        @pl.when(ctx + j >= RANGES)
        def _():
            dkvr[:, j * 128 : (j + 1) * 128] = jnp.zeros((256, 128), BF16)

    wall[pl.ds(pl.multiple_of(core * ROWS, 16), ROWS), :] = w_ref[...]
    for b in range(D // 128):
        xt[b * 128 : (b + 1) * 128, :] = x_ref[:, b * 128 : (b + 1) * 128].T
    pl.semaphore_wait(barrier, RANGES + zn - 1)

    def own_rows(i, n, mult):
        return pl.ds(pl.multiple_of(i * n, mult), n)

    def meta_copy(j):
        return remote(meta.at[ctx], meta.at[ctx], meta_s.at[j - 1], meta_r.at[j - 1], at(dp, (ctx + j) % RANGES))

    def meta_in(j):
        slot = (ctx + RANGES - j) % RANGES
        return remote(meta.at[slot], meta.at[slot], meta_s.at[j - 1], meta_r.at[j - 1], sibling)

    w_mine = own_rows(core, ROWS, 16)
    w_theirs = own_rows(1 - core, ROWS, 16)
    w_copy = remote(wall.at[w_mine, :], wall.at[w_mine, :], w_s, w_r, sibling)
    w_copy.start()
    x_copies = []
    for j in range(1, CHIPS):
        other = (chip + j) % CHIPS
        copy = remote(
            xt.at[own_rows(other, WIDE, 16), :], xall.at[:, lanes(chip)], x_s.at[j - 1], x_r.at[j - 1], chip_at(j)
        )
        copy.start()
        x_copies.append(copy)

    def meta_start(j, carry):
        meta_copy(j).start()
        return carry

    lax.fori_loop(1, RANGES, meta_start, 0)
    xall[:, lanes(chip)] = xt[own_rows(chip, WIDE, 16), :]

    for h in range(2):
        block = g_ref[:, h * 128 : (h + 1) * 128]
        gs[h * 128 : (h + 1) * 128, :] = block
        gt[:, h * 128 : (h + 1) * 128] = block.T

    remote(wall.at[w_theirs, :], wall.at[w_theirs, :], w_s, w_r, sibling).wait_recv()

    acc[...] = tn(wall[...], xall[:, lanes(chip)])
    p_copies = []
    for j in range(1, CHIPS):
        other = (chip + CHIPS - j) % CHIPS
        remote(
            xt.at[own_rows(other, WIDE, 16), :], xall.at[:, lanes(other)], x_s.at[j - 1], x_r.at[j - 1], chip_at(j)
        ).wait_recv()
        part[j - 1] = tn(wall[...], xall[:, lanes(other)]).astype(BF16)
        copy = remote(
            part.at[j - 1], projr.at[j - 1], p_s.at[j - 1], p_r.at[j - 1], chip_at(CHIPS - j)
        )
        copy.start()
        p_copies.append(copy)

    def meta_wait(j, carry):
        meta_in(j).wait_recv()
        return carry

    lax.fori_loop(1, RANGES, meta_wait, 0)
    lane = lax.broadcasted_iota(jnp.int32, (8, 128), 1).astype(F32)
    begin = jnp.zeros((8, 128), F32)
    for r in range(RANGES):
        doc = jnp.broadcast_to(meta[r, 0:1, :], (8, 128)).astype(F32)
        length = jnp.broadcast_to(meta[r, 1:2, :], (8, 128)).astype(F32)
        keypos[r] = jnp.where(lane < length, begin + lane + DOC_STEP * doc, FAR)
        keypos[RANGES + r] = begin + lane
        begin = begin + length
    angle = freq_ref[...] * jnp.broadcast_to(keypos[RANGES + ctx][0:1, :], (64, 128))
    cosine, sine = jnp.cos(angle), jnp.sin(angle)
    own = jnp.broadcast_to(keypos[ctx][0:1, :], (128, 128)).T
    qpos = jnp.where(own >= 0.5 * FAR, -FAR, own)

    for j in range(1, CHIPS):
        remote(part.at[j - 1], projr.at[j - 1], p_s.at[j - 1], p_r.at[j - 1], chip_at(j)).wait_recv()
    for n in range(4):
        rows = slice(n * 128, (n + 1) * 128)
        total = acc[rows, :]
        for j in range(1, CHIPS):
            total = total + projr[j - 1, rows, :].astype(F32)
        if n < 3:
            u, v = total[:64], total[64:]
            total = jnp.concatenate([u * cosine - v * sine, v * cosine + u * sine], axis=0)
        low = total.astype(BF16)
        if n < 2:
            qt[:, rows] = low
            qs[rows, :] = low.astype(F32).T.astype(BF16)
        else:
            kvt[(n - 2) * 128 : (n - 1) * 128, 0:128] = low

    def kv_copy(j, target):
        return remote(
            kvt.at[:, 0:128], kvt.at[:, j * 128 : (j + 1) * 128], kv_s.at[j - 1], kv_r.at[j - 1], at(dp, target)
        )

    for j in range(1, SLOTS):
        @pl.when(ctx + j < RANGES)
        def _():
            kv_copy(j, ctx + j).start()

    for j in range(1, SLOTS):
        @pl.when(ctx - j >= 0)
        def _():
            kv_copy(j, ctx - j).wait_recv()

    sbuf[...] = nn(qs[...], kvt[0:128, :])
    dbuf[...] = nn(gs[...], kvt[128:256, :])
    kpos = []
    for j in range(SLOTS):
        block = keypos[(ctx + RANGES - j) % RANGES][0:1, :]
        kpos.append(jnp.where(ctx - j >= 0, block, jnp.full((1, 128), FAR, F32)))
    kpos = jnp.concatenate(kpos, axis=1)
    step = 16
    for i in range(256 // step):
        rows = slice(i * step, (i + 1) * step)
        qrow = (i * step) % 128
        gap = qpos[qrow : qrow + step, 0:1] - kpos
        allowed = (gap >= 0.0) & (gap < float(WINDOW))
        s = jnp.where(allowed, sbuf[rows, :] * SCALE, NEG)
        dots = dbuf[rows, :]
        top = jnp.maximum(jnp.max(s, axis=1, keepdims=True), 0.1 * NEG)
        e = jnp.exp(s - top)
        total = jnp.sum(e, axis=1, keepdims=True)
        weighted = jnp.sum(e * dots, axis=1, keepdims=True)
        inverse = 1.0 / jnp.where(total > 0.0, total, 1.0)
        prob = e * inverse
        pbuf[rows, :] = prob.astype(BF16)
        dsbuf[rows, :] = (prob * (dots - weighted * inverse)).astype(BF16)

    dk = nn(qt[...], dsbuf[...]) * SCALE
    dv = nn(gt[...], pbuf[...])
    dkvs[0:128, :] = dk.astype(BF16)
    dkvs[128:256, :] = dv.astype(BF16)
    acc[0:128, :] = dk[:, 0:128]
    acc[128:256, :] = dv[:, 0:128]

    def dk_copy(j, target):
        span = slice(j * 128, (j + 1) * 128)
        return remote(dkvs.at[:, span], dkvr.at[:, span], dk_s.at[j - 1], dk_r.at[j - 1], at(dp, target))

    for j in range(1, SLOTS):
        @pl.when(ctx - j >= 0)
        def _():
            dk_copy(j, ctx - j).start()

    for h in range(2):
        dq = nt(kvt[0:128, :], dsbuf[h * 128 : (h + 1) * 128, :]) * SCALE
        u, v = dq[:64], dq[64:]
        dq = jnp.concatenate([u * cosine + v * sine, v * cosine - u * sine], axis=0)
        dpt[h * 128 : (h + 1) * 128, lanes(chip)] = dq.astype(BF16)

    for j in range(1, SLOTS):
        @pl.when(ctx + j < RANGES)
        def _():
            dk_copy(j, ctx + j).wait_recv()

    dk = acc[0:128, :]
    dv = acc[128:256, :]
    for j in range(1, SLOTS):
        span = slice(j * 128, (j + 1) * 128)
        dk = dk + dkvr[0:128, span].astype(F32)
        dv = dv + dkvr[128:256, span].astype(F32)
    u, v = dk[:64], dk[64:]
    dk = jnp.concatenate([u * cosine + v * sine, v * cosine - u * sine], axis=0)
    dpt[256:384, lanes(chip)] = dk.astype(BF16)
    dpt[384:512, lanes(chip)] = dv.astype(BF16)

    def dp_copy(j, slot, dev):
        return remote(dpt.at[:, lanes(slot)], dpt.at[:, lanes(slot)], dp_s.at[j - 1], dp_r.at[j - 1], dev)

    for j in range(1, CHIPS):
        dp_copy(j, chip, chip_at(j)).start()
    dxt[own_rows(chip, WIDE, 16), :] = nn(wall[...], dpt[:, lanes(chip)]).astype(BF16)
    for j in range(1, CHIPS):
        dp_copy(j, (chip + CHIPS - j) % CHIPS, chip_at(j)).wait_recv()

    a1s[...] = nt(dpt[...], xall[w_theirs, :]).astype(BF16)
    a1_copy = remote(a1s, a1r, a1_s, a1_r, sibling)
    a1_copy.start()
    tb[...] = nt(dpt[...], xall[w_mine, :])
    a1_copy.wait_recv()
    tb[...] = tb[...] + a1r[...].astype(F32)
    a2s[...] = tb[own_rows(1 - yl, 256, 256), :].astype(BF16)
    a2_copy = remote(a2s, a2r, a2_s, a2_r, ypair)
    a2_copy.start()

    dx_copies = []
    for j in range(1, CHIPS):
        other = (chip + j) % CHIPS
        dxs[j - 1] = nn(wall[...], dpt[:, lanes(other)]).astype(BF16)
        copy = remote(
            dxs.at[j - 1], dxt.at[own_rows(chip, WIDE, 16), :], dx_s.at[j - 1], dx_r.at[j - 1], chip_at(j)
        )
        copy.start()
        dx_copies.append(copy)

    a2_copy.wait_recv()
    ub[...] = tb[own_rows(yl, 256, 256), :] + a2r[...].astype(F32)
    a3s[...] = ub[...].astype(BF16)

    def a3_copy(j):
        other = (zi + j) % zn
        return remote(a3s.at[own_rows(other, rz, 16), :], a3r.at[j - 1], a3_s.at[j - 1], a3_r.at[j - 1], zpeer(j))

    def a3_start(j, carry):
        a3_copy(j).start()
        return carry

    def a3_wait(j, carry):
        a3_copy(j).wait_recv()
        return carry + a3r[j - 1].astype(F32)

    lax.fori_loop(1, zn, a3_start, 0)

    for j in range(1, CHIPS):
        other = (chip + CHIPS - j) % CHIPS
        remote(
            dxs.at[j - 1], dxt.at[own_rows(other, WIDE, 16), :], dx_s.at[j - 1], dx_r.at[j - 1], chip_at(j)
        ).wait_recv()
    for b in range(D // 128):
        dx_ref[:, b * 128 : (b + 1) * 128] = dxt[b * 128 : (b + 1) * 128, :].T

    total = lax.fori_loop(1, zn, a3_wait, ub[own_rows(zi, rz, 16), :])
    mine = own_rows(yl * zn + zi, rz, 16)
    ag[mine, :] = total.astype(BF16)

    def ag_copy(j, place, dev):
        span = own_rows(place, rz, 16)
        return remote(ag.at[span, :], ag.at[span, :], ag_s.at[j - 1], ag_r.at[j - 1], dev)

    def f_copy(j, place):
        span = own_rows(place, rz, 16)
        return remote(ag.at[span, :], ag.at[span, :], f_s.at[j], f_r.at[j], ypair)

    def ag_start(j, carry):
        ag_copy(j, yl * zn + zi, zpeer(j)).start()
        return carry

    lax.fori_loop(1, zn, ag_start, 0)
    f_copy(0, yl * zn + zi).start()

    def ag_forward(j, carry):
        place = yl * zn + (zi + zn - j) % zn
        ag_copy(j, place, ypair).wait_recv()
        f_copy(j, place).start()
        return carry

    lax.fori_loop(1, zn, ag_forward, 0)

    def f_wait(j, carry):
        f_copy(j, (1 - yl) * zn + (zi + zn - j) % zn).wait_recv()
        return carry

    lax.fori_loop(0, zn, f_wait, 0)
    dwt_ref[...] = ag[...].astype(F32)

    w_copy.wait_send()
    for copy in x_copies + p_copies + dx_copies:
        copy.wait_send()

    def meta_sent(j, carry):
        meta_copy(j).wait_send()
        return carry

    lax.fori_loop(1, RANGES, meta_sent, 0)
    for j in range(1, SLOTS):
        @pl.when(ctx + j < RANGES)
        def _():
            kv_copy(j, ctx + j).wait_send()

        @pl.when(ctx - j >= 0)
        def _():
            dk_copy(j, ctx - j).wait_send()

    for j in range(1, CHIPS):
        dp_copy(j, chip, chip_at(j)).wait_send()
    a1_copy.wait_send()
    a2_copy.wait_send()

    def z_sent(j, carry):
        a3_copy(j).wait_send()
        ag_copy(j, yl * zn + zi, zpeer(j)).wait_send()
        return carry

    lax.fori_loop(1, zn, z_sent, 0)

    def f_sent(j, carry):
        f_copy(j, yl * zn + (zi + zn - j) % zn).wait_send()
        return carry

    lax.fori_loop(0, zn, f_sent, 0)


def body(zn, hidden_in, w_qkv, d_attn, range_len, doc_ids):
    rz = 256 // zn
    freqs = 10000.0 ** (-(np.arange(64, dtype=np.float64) * 2.0) / HD)
    freqs = jnp.asarray(np.broadcast_to(freqs[:, None], (64, 128)).astype(np.float32))
    vmem = pl.BlockSpec(memory_space=pltpu.VMEM)
    dma = pltpu.SemaphoreType.DMA
    scratch = [
        pltpu.VMEM((RANGES, 8, 128), jnp.int32),
        pltpu.VMEM((2 * RANGES, 8, 128), F32),
        pltpu.VMEM((D, 128), BF16),
        pltpu.VMEM((WIDE, CHIPS * 128), BF16),
        pltpu.VMEM((WIDE, QKV), BF16),
        pltpu.VMEM((CHIPS - 1, QKV, 128), BF16),
        pltpu.VMEM((CHIPS - 1, QKV, 128), BF16),
        pltpu.VMEM((QKV, 128), F32),
        pltpu.VMEM((128, 256), BF16),
        pltpu.VMEM((256, 128), BF16),
        pltpu.VMEM((256, 128), BF16),
        pltpu.VMEM((128, 256), BF16),
        pltpu.VMEM((256, SLOTS * 128), BF16),
        pltpu.VMEM((256, SLOTS * 128), F32),
        pltpu.VMEM((256, SLOTS * 128), F32),
        pltpu.VMEM((256, SLOTS * 128), BF16),
        pltpu.VMEM((256, SLOTS * 128), BF16),
        pltpu.VMEM((256, SLOTS * 128), BF16),
        pltpu.VMEM((256, SLOTS * 128), BF16),
        pltpu.VMEM((QKV, CHIPS * 128), BF16),
        pltpu.VMEM((CHIPS - 1, WIDE, 128), BF16),
        pltpu.VMEM((D, 128), BF16),
        pltpu.VMEM((QKV, ROWS), BF16),
        pltpu.VMEM((QKV, ROWS), BF16),
        pltpu.VMEM((QKV, ROWS), F32),
        pltpu.VMEM((256, ROWS), BF16),
        pltpu.VMEM((256, ROWS), BF16),
        pltpu.VMEM((256, ROWS), F32),
        pltpu.VMEM((256, ROWS), BF16),
        pltpu.VMEM((zn - 1, rz, ROWS), BF16),
        pltpu.VMEM((QKV, ROWS), BF16),
        dma((RANGES - 1,)), dma((RANGES - 1,)),
        dma, dma,
        dma((CHIPS - 1,)), dma((CHIPS - 1,)),
        dma((CHIPS - 1,)), dma((CHIPS - 1,)),
        dma((REACH,)), dma((REACH,)),
        dma((REACH,)), dma((REACH,)),
        dma((CHIPS - 1,)), dma((CHIPS - 1,)),
        dma((CHIPS - 1,)), dma((CHIPS - 1,)),
        dma, dma,
        dma, dma,
        dma((zn - 1,)), dma((zn - 1,)),
        dma((zn - 1,)), dma((zn - 1,)),
        dma((zn,)), dma((zn,)),
    ]
    d_x, d_wt = pl.pallas_call(
        functools.partial(kernel, zn),
        name="block_backward",
        out_shape=(jax.ShapeDtypeStruct((CAP, D), BF16), jax.ShapeDtypeStruct((QKV, ROWS), F32)),
        in_specs=[vmem] * 6,
        out_specs=(vmem, vmem),
        scratch_shapes=scratch,
        compiler_params=pltpu.CompilerParams(
            collective_id=0, has_side_effects=True, vmem_limit_bytes=50 * 1024 * 1024
        ),
    )(hidden_in[0], w_qkv, d_attn[0], range_len, doc_ids, freqs)
    return d_x[None], d_wt.T


def solution(mesh):
    return jax.shard_map(
        functools.partial(body, mesh.shape["dp"] // 2),
        mesh=mesh,
        in_specs=(
            P("dp", "ctx", None),
            P("ctx", None),
            P("dp", "ctx", None),
            P("dp", "ctx"),
            P("dp", "ctx"),
        ),
        out_specs=(P("dp", "ctx", None), P("ctx", None)),
        check_vma=False,
    )
```

time: 600 us -> 149 us (0.25)
  the two profiles are of different devices: /device:TPU:2 before, /device:TPU:18 now
where the time goes in v1:
time: 149 us
  Pallas kernels  141 us (95%)
  local copies, waits for them, and re-layouts  6.74 us (5%)
    pallas_call x1, Pallas kernels, body(): pl.pallas_call(functools.partial(kernel, zn), name='block_backward', out_...  141 us
    unnamed x12, local copies, waits for them, and re-layouts  6.74 us

profile of v1, /device:TPU:18, one launch (start us, length us, event | category | flops | bytes accessed | tf_op | source)
XLA Modules:
  0.0 148.6 jit_solution(11510507871405641568)
XLA Ops:
  1.3 0.0 copy-start
  1.3 1.3 copy-done
  2.6 0.0 copy-start.1
  2.6 1.0 copy-done.1
  3.6 0.0 copy-start.2
  3.6 0.8 copy-done.2
  4.4 0.0 copy-start.3
  4.4 0.8 copy-done.3
  5.2 0.0 copy-start.4
  5.2 0.7 copy-done.4
  5.8 140.6 %block_backward.1 = (bf16[128,5376]{1,0:T(8,128)(2,1)S(1)}, f32[512,336]{1,0:T(8,128)S(1)}) custom-call(bf16[128,5376]{1,0:T(8,128)(2,1)S(1)} %bitcast.4, bf16[336,512]{1,0:T(8,128)(2,1)S(1)} %copy-done.1, bf16[128,256]{1,0:T(8,128)(2,1)S(1)} %bitcast.7, s32[1,1]{1,0:T(1,128)S(6)} %copy.10.len_ref, s32[1,128]{1,0:T(1,128)S(1)} %copy-done.4, ...), custom_call_target="tpu_custom_call" | custom-call | tf_op jit(solution)/shard_map/block_backward/pallas_call | solution.py:453
  146.4 1.1 copy.8
  147.5 1.1 copy.11
Async XLA Ops:
  1.3 1.3 copy-start
  2.6 1.0 copy-start.1
  3.6 0.8 copy-start.2
  4.4 0.8 copy-start.3
  5.2 0.7 copy-start.4

commit v2 on v1

v2 whole, which is shorter than its diff:
```python
import functools

import jax
import jax.numpy as jnp
import numpy as np
from jax import lax
from jax.experimental import pallas as pl
from jax.experimental.pallas import tpu as pltpu
from jax.sharding import PartitionSpec as P

HD = 128
WINDOW = 1024
CAP = 128
D = 5376
QKV = 512
RANGES = 16
CHIPS = 8
ROWS = D // RANGES
WIDE = D // CHIPS
REACH = 11
SLOTS = REACH + 1
DOC_STEP = 4096.0
FAR = 1.0e6
NEG = -1.0e30
SCALE = 168.0 ** (-0.5)
MESH = pl.DeviceIdType.MESH
F32 = jnp.float32
BF16 = jnp.bfloat16


def nt(a, b):
    return lax.dot_general(a, b, (((1,), (1,)), ((), ())), preferred_element_type=F32)


def tn(a, b):
    return lax.dot_general(a, b, (((0,), (0,)), ((), ())), preferred_element_type=F32)


def nn(a, b):
    return jnp.dot(a, b, preferred_element_type=F32)


def kernel(
    zn,
    x_ref, w_ref, g_ref, len_ref, doc_ref, freq_ref,
    dx_ref, dwt_ref,
    xv, gv, lenv, docv, freqv,
    meta, keypos, xt, xall, wall, part, projr, proj, dkv, qt, qs, gs, gt, kvt, sbuf, dbuf, pbuf, dsbuf,
    dkvs, dkvr, dpt, dxs, dxt, a1s, a1r, tb, a2s, a2r, ub, a3s, a3r, u2, b3s, b3r, ag,
    in_s, meta_s, meta_r, w_s, w_r, x_s, x_r, p_s, p_r, kv_s, kv_r, dk_s, dk_r, dp_s, dp_r, dx_s, dx_r,
    a1_s, a1_r, a2_s, a2_r, a3_s, a3_r, b3_s, b3_r, c_s, c_r, d_s, d_r, f_s, f_r,
):
    dp = lax.axis_index("dp")
    ctx = lax.axis_index("ctx")
    zi, yl = dp % zn, dp // zn
    chip, core = ctx // 2, ctx % 2
    nb = 4 if zn == 16 else 2
    na = zn // nb
    za, zb = zi // nb, zi % nb

    def at(d, c):
        return {"dp": d, "ctx": c}

    def remote(src, dst, ss, rs, dev):
        return pltpu.make_async_remote_copy(
            src_ref=src, dst_ref=dst, send_sem=ss, recv_sem=rs, device_id=dev, device_id_type=MESH
        )

    def lanes(i):
        return pl.ds(pl.multiple_of(i * 128, 128), 128)

    def chip_at(j):
        return at(dp, ((chip + j) % CHIPS) * 2 + core)

    sibling = at(dp, chip * 2 + (1 - core))
    ypair = at((1 - yl) * zn + zi, ctx)

    def bpeer(j):
        return at(yl * zn + za * nb + (zb + j) % nb, ctx)

    def apeer(j):
        return at(yl * zn + ((za + j) % na) * nb + zb, ctx)

    pending = []
    barrier = pltpu.get_barrier_semaphore()

    def greet_ctx(j, carry):
        pl.semaphore_signal(barrier, inc=1, device_id=at(dp, (ctx + j) % RANGES), device_id_type=MESH)
        return carry

    loads = [
        pltpu.make_async_copy(x_ref.at[0], xv, in_s.at[0]),
        pltpu.make_async_copy(w_ref, wall.at[pl.ds(pl.multiple_of(core * ROWS, 16), ROWS), :], in_s.at[1]),
        pltpu.make_async_copy(g_ref.at[0], gv, in_s.at[2]),
        pltpu.make_async_copy(len_ref, lenv, in_s.at[3]),
        pltpu.make_async_copy(doc_ref, docv, in_s.at[4]),
        pltpu.make_async_copy(freq_ref, freqv, in_s.at[5]),
    ]
    for load in loads:
        load.start()
    for j in range(1, na):
        pl.semaphore_signal(barrier, inc=1, device_id=apeer(j), device_id_type=MESH)
    for j in range(1, nb):
        pl.semaphore_signal(barrier, inc=1, device_id=bpeer(j), device_id_type=MESH)
    pl.semaphore_signal(barrier, inc=1, device_id=ypair, device_id_type=MESH)
    lax.fori_loop(1, RANGES, greet_ctx, 0)
    for load in loads:
        load.wait()

    row = lax.broadcasted_iota(jnp.int32, (8, 128), 0)
    meta[ctx] = jnp.where(
        row == 0,
        jnp.broadcast_to(docv[...], (8, 128)),
        jnp.broadcast_to(lenv[...], (8, 128)),
    )
    for j in range(1, SLOTS):
        @pl.when(ctx - j < 0)
        def _():
            kvt[:, j * 128 : (j + 1) * 128] = jnp.zeros((256, 128), BF16)

        @pl.when(ctx + j >= RANGES)
        def _():
            dkvr[:, j * 128 : (j + 1) * 128] = jnp.zeros((256, 128), BF16)

    for b in range(D // 128):
        xt[b * 128 : (b + 1) * 128, :] = xv[:, b * 128 : (b + 1) * 128].T
    pl.semaphore_wait(barrier, RANGES + na + nb - 2)

    def own_rows(i, n, mult):
        return pl.ds(pl.multiple_of(i * n, mult), n)

    def meta_copy(j):
        return remote(meta.at[ctx], meta.at[ctx], meta_s.at[j - 1], meta_r.at[j - 1], at(dp, (ctx + j) % RANGES))

    def meta_in(j):
        slot = (ctx + RANGES - j) % RANGES
        return remote(meta.at[slot], meta.at[slot], meta_s.at[j - 1], meta_r.at[j - 1], sibling)

    w_mine = own_rows(core, ROWS, 16)
    w_theirs = own_rows(1 - core, ROWS, 16)
    w_copy = remote(wall.at[w_mine, :], wall.at[w_mine, :], w_s, w_r, sibling)
    w_copy.start()
    pending.append(w_copy.wait_send)
    for j in range(1, CHIPS):
        other = (chip + j) % CHIPS
        copy = remote(
            xt.at[own_rows(other, WIDE, 16), :], xall.at[:, lanes(chip)], x_s.at[j - 1], x_r.at[j - 1], chip_at(j)
        )
        copy.start()
        pending.append(copy.wait_send)

    def meta_start(j, carry):
        meta_copy(j).start()
        return carry

    lax.fori_loop(1, RANGES, meta_start, 0)

    def meta_sent(j, carry):
        meta_copy(j).wait_send()
        return carry

    pending.append(lambda: lax.fori_loop(1, RANGES, meta_sent, 0))
    xall[:, lanes(chip)] = xt[own_rows(chip, WIDE, 16), :]

    for h in range(2):
        block = gv[:, h * 128 : (h + 1) * 128]
        gs[h * 128 : (h + 1) * 128, :] = block
        gt[:, h * 128 : (h + 1) * 128] = block.T

    remote(wall.at[w_theirs, :], wall.at[w_theirs, :], w_s, w_r, sibling).wait_recv()

    proj[...] = tn(xall[:, lanes(chip)], wall[...])
    for j in range(1, CHIPS):
        other = (chip + CHIPS - j) % CHIPS
        remote(
            xt.at[own_rows(other, WIDE, 16), :], xall.at[:, lanes(other)], x_s.at[j - 1], x_r.at[j - 1], chip_at(j)
        ).wait_recv()
        part[j - 1] = tn(xall[:, lanes(other)], wall[...]).astype(BF16)
        copy = remote(
            part.at[j - 1], projr.at[j - 1], p_s.at[j - 1], p_r.at[j - 1], chip_at(CHIPS - j)
        )
        copy.start()
        pending.append(copy.wait_send)

    def meta_wait(j, carry):
        meta_in(j).wait_recv()
        return carry

    lax.fori_loop(1, RANGES, meta_wait, 0)
    lane = lax.broadcasted_iota(jnp.int32, (8, 128), 1).astype(F32)
    begin = jnp.zeros((8, 128), F32)
    for r in range(RANGES):
        doc = jnp.broadcast_to(meta[r, 0:1, :], (8, 128)).astype(F32)
        length = jnp.broadcast_to(meta[r, 1:2, :], (8, 128)).astype(F32)
        keypos[r] = jnp.where(lane < length, begin + lane + DOC_STEP * doc, FAR)
        keypos[RANGES + r] = begin + lane
        begin = begin + length
    angle = freqv[...] * jnp.broadcast_to(keypos[RANGES + ctx][0:1, :], (64, 128))
    cosine, sine = jnp.cos(angle), jnp.sin(angle)
    own = jnp.broadcast_to(keypos[ctx][0:1, :], (128, 128)).T
    qpos = jnp.where(own >= 0.5 * FAR, -FAR, own)

    for j in range(1, CHIPS):
        remote(part.at[j - 1], projr.at[j - 1], p_s.at[j - 1], p_r.at[j - 1], chip_at(j)).wait_recv()
    for n in range(4):
        rows = slice(n * 128, (n + 1) * 128)
        total = proj[:, rows]
        for j in range(1, CHIPS):
            total = total + projr[j - 1, :, rows].astype(F32)
        total = total.T
        if n < 3:
            u, v = total[:64], total[64:]
            total = jnp.concatenate([u * cosine - v * sine, v * cosine + u * sine], axis=0)
        low = total.astype(BF16)
        if n < 2:
            qt[:, rows] = low
            qs[rows, :] = low.astype(F32).T.astype(BF16)
        else:
            kvt[(n - 2) * 128 : (n - 1) * 128, 0:128] = low

    def kv_copy(j, target):
        return remote(
            kvt.at[:, 0:128], kvt.at[:, j * 128 : (j + 1) * 128], kv_s.at[j - 1], kv_r.at[j - 1], at(dp, target)
        )

    for j in range(1, SLOTS):
        @pl.when(ctx + j < RANGES)
        def _():
            kv_copy(j, ctx + j).start()

    def kv_sent():
        for j in range(1, SLOTS):
            @pl.when(ctx + j < RANGES)
            def _():
                kv_copy(j, ctx + j).wait_send()

    pending.append(kv_sent)

    for j in range(1, SLOTS):
        @pl.when(ctx - j >= 0)
        def _():
            kv_copy(j, ctx - j).wait_recv()

    sbuf[...] = nn(qs[...], kvt[0:128, :])
    dbuf[...] = nn(gs[...], kvt[128:256, :])
    kpos = []
    for j in range(SLOTS):
        block = keypos[(ctx + RANGES - j) % RANGES][0:1, :]
        kpos.append(jnp.where(ctx - j >= 0, block, jnp.full((1, 128), FAR, F32)))
    kpos = jnp.concatenate(kpos, axis=1)
    step = 16
    for i in range(256 // step):
        rows = slice(i * step, (i + 1) * step)
        qrow = (i * step) % 128
        gap = qpos[qrow : qrow + step, 0:1] - kpos
        allowed = (gap >= 0.0) & (gap < float(WINDOW))
        s = jnp.where(allowed, sbuf[rows, :] * SCALE, NEG)
        dots = dbuf[rows, :]
        top = jnp.maximum(jnp.max(s, axis=1, keepdims=True), 0.1 * NEG)
        e = jnp.exp(s - top)
        total = jnp.sum(e, axis=1, keepdims=True)
        weighted = jnp.sum(e * dots, axis=1, keepdims=True)
        inverse = 1.0 / jnp.where(total > 0.0, total, 1.0)
        prob = e * inverse
        pbuf[rows, :] = prob.astype(BF16)
        dsbuf[rows, :] = (prob * (dots - weighted * inverse)).astype(BF16)

    dk = nn(qt[...], dsbuf[...]) * SCALE
    dv = nn(gt[...], pbuf[...])
    dkvs[0:128, :] = dk.astype(BF16)
    dkvs[128:256, :] = dv.astype(BF16)
    dkv[0:128, :] = dk[:, 0:128]
    dkv[128:256, :] = dv[:, 0:128]

    def dk_copy(j, target):
        span = slice(j * 128, (j + 1) * 128)
        return remote(dkvs.at[:, span], dkvr.at[:, span], dk_s.at[j - 1], dk_r.at[j - 1], at(dp, target))

    for j in range(1, SLOTS):
        @pl.when(ctx - j >= 0)
        def _():
            dk_copy(j, ctx - j).start()

    def dk_sent():
        for j in range(1, SLOTS):
            @pl.when(ctx - j >= 0)
            def _():
                dk_copy(j, ctx - j).wait_send()

    pending.append(dk_sent)

    for h in range(2):
        dq = nt(kvt[0:128, :], dsbuf[h * 128 : (h + 1) * 128, :]) * SCALE
        u, v = dq[:64], dq[64:]
        dq = jnp.concatenate([u * cosine + v * sine, v * cosine - u * sine], axis=0)
        dpt[h * 128 : (h + 1) * 128, lanes(chip)] = dq.astype(BF16)

    def dp_copy(half, j, slot, dev):
        part_ref = dpt.at[half * 256 : (half + 1) * 256, lanes(slot)]
        return remote(part_ref, part_ref, dp_s.at[half, j - 1], dp_r.at[half, j - 1], dev)

    def dp_send(half):
        for j in range(1, CHIPS):
            copy = dp_copy(half, j, chip, chip_at(j))
            copy.start()
            pending.append(copy.wait_send)

    def dp_wait(half):
        for j in range(1, CHIPS):
            dp_copy(half, j, (chip + CHIPS - j) % CHIPS, chip_at(j)).wait_recv()

    dp_send(0)
    for j in range(1, SLOTS):
        @pl.when(ctx + j < RANGES)
        def _():
            dk_copy(j, ctx + j).wait_recv()

    dk = dkv[0:128, :]
    dv = dkv[128:256, :]
    for j in range(1, SLOTS):
        span = slice(j * 128, (j + 1) * 128)
        dk = dk + dkvr[0:128, span].astype(F32)
        dv = dv + dkvr[128:256, span].astype(F32)
    u, v = dk[:64], dk[64:]
    dk = jnp.concatenate([u * cosine + v * sine, v * cosine - u * sine], axis=0)
    dpt[256:384, lanes(chip)] = dk.astype(BF16)
    dpt[384:512, lanes(chip)] = dv.astype(BF16)

    dp_send(1)

    def sum_rows(half):
        return dpt[half * 256 : (half + 1) * 256, :]

    def one(copy):
        copy.start()
        pending.append(copy.wait_send)

    def a1_copy(half):
        return remote(a1s.at[half], a1r.at[half], a1_s.at[half], a1_r.at[half], sibling)

    def a2_copy(half):
        return remote(a2s.at[half], a2r.at[half], a2_s.at[half], a2_r.at[half], ypair)

    def group(i):
        return pl.ds(i * na, na)

    def a3_copy(half, j):
        src = a3s.at[half, group((zb + j) % nb)]
        return remote(src, a3r.at[half, j - 1], a3_s.at[half, j - 1], a3_r.at[half, j - 1], bpeer(j))

    def b3_copy(half, j):
        src = b3s.at[half, pl.ds((za + j) % na, 1)]
        return remote(src, b3r.at[half, j - 1], b3_s.at[half, j - 1], b3_r.at[half, j - 1], apeer(j))

    def c_copy(half, j, place):
        chunk = ag.at[half, yl, pl.ds(place, 1)]
        return remote(chunk, chunk, c_s.at[half, j - 1], c_r.at[half, j - 1], apeer(j))

    def d_copy(half, j, place):
        chunk = ag.at[half, yl, group(place)]
        return remote(chunk, chunk, d_s.at[half, j - 1], d_r.at[half, j - 1], bpeer(j))

    def f_copy(half, j, side, place):
        chunk = ag.at[half, side, group(place)]
        return remote(chunk, chunk, f_s.at[half, j], f_r.at[half, j], ypair)

    def step1(half):
        a1s[half] = nt(sum_rows(half), xall[w_theirs, :]).astype(BF16)
        one(a1_copy(half))
        tb[half] = nt(sum_rows(half), xall[w_mine, :])

    def step2(half):
        a1_copy(half).wait_recv()
        tb[half] = tb[half] + a1r[half].astype(F32)
        a2s[half] = tb[half, own_rows(1 - yl, 128, 128), :].astype(BF16)
        one(a2_copy(half))

    def step3(half):
        a2_copy(half).wait_recv()
        total = tb[half, own_rows(yl, 128, 128), :] + a2r[half].astype(F32)
        for i in range(16):
            ub[half, i] = total[i * 8 : (i + 1) * 8, :]
            a3s[half, i] = total[i * 8 : (i + 1) * 8, :].astype(BF16)
        for j in range(1, nb):
            one(a3_copy(half, j))

    def step4(half):
        total = ub[half, group(zb)]
        for j in range(1, nb):
            a3_copy(half, j).wait_recv()
            total = total + a3r[half, j - 1].astype(F32)
        u2[half] = total
        b3s[half] = total.astype(BF16)
        for j in range(1, na):
            one(b3_copy(half, j))

    def step5(half):
        total = u2[half, pl.ds(za, 1)]
        for j in range(1, na):
            b3_copy(half, j).wait_recv()
            total = total + b3r[half, j - 1].astype(F32)
        place = zb * na + za
        ag[half, yl, pl.ds(place, 1)] = total.astype(BF16)
        for j in range(1, na):
            one(c_copy(half, j, place))

    def step6(half):
        for j in range(1, na):
            c_copy(half, j, zb * na + (za + na - j) % na).wait_recv()
        for j in range(1, nb):
            one(d_copy(half, j, zb))
        one(f_copy(half, 0, yl, zb))

    def step7(half):
        for j in range(1, nb):
            place = (zb + nb - j) % nb
            d_copy(half, j, place).wait_recv()
            one(f_copy(half, j, yl, place))

    def step8(half):
        for j in range(nb):
            f_copy(half, j, 1 - yl, (zb + nb - j) % nb).wait_recv()
        for side in range(2):
            for i in range(16):
                low = half * 256 + side * 128 + i * 8
                dwt_ref[low : low + 8, :] = ag[half, side, i].astype(F32)

    dp_wait(0)
    step1(0)
    step2(0)
    step3(0)
    dp_wait(1)
    step1(1)
    step2(1)

    for j in range(1, CHIPS):
        other = (chip + j) % CHIPS
        dxs[j - 1] = nn(wall[...], dpt[:, lanes(other)]).astype(BF16)
        one(
            remote(dxs.at[j - 1], dxt.at[own_rows(chip, WIDE, 16), :], dx_s.at[j - 1], dx_r.at[j - 1], chip_at(j))
        )
    step4(0)
    step3(1)
    dxt[own_rows(chip, WIDE, 16), :] = nn(wall[...], dpt[:, lanes(chip)]).astype(BF16)
    step5(0)
    step4(1)
    step6(0)
    step5(1)
    step7(0)
    step6(1)
    for j in range(1, CHIPS):
        other = (chip + CHIPS - j) % CHIPS
        remote(
            dxs.at[j - 1], dxt.at[own_rows(other, WIDE, 16), :], dx_s.at[j - 1], dx_r.at[j - 1], chip_at(j)
        ).wait_recv()
    step7(1)
    for b in range(D // 128):
        dx_ref[:, b * 128 : (b + 1) * 128] = dxt[b * 128 : (b + 1) * 128, :].T
    step8(0)
    step8(1)

    for left in pending:
        left()


def body(zn, hidden_in, w_qkv, d_attn, range_len, doc_ids):
    nb = 4 if zn == 16 else 2
    na = zn // nb
    freqs = 10000.0 ** (-(np.arange(64, dtype=np.float64) * 2.0) / HD)
    freqs = jnp.asarray(np.broadcast_to(freqs[:, None], (64, 128)).astype(np.float32))
    vmem = pl.BlockSpec(memory_space=pltpu.VMEM)
    dma = pltpu.SemaphoreType.DMA
    scratch = [
        pltpu.VMEM((CAP, D), BF16),
        pltpu.VMEM((CAP, 256), BF16),
        pltpu.VMEM((1, 1), jnp.int32),
        pltpu.VMEM((1, 128), jnp.int32),
        pltpu.VMEM((64, 128), F32),
        pltpu.VMEM((RANGES, 8, 128), jnp.int32),
        pltpu.VMEM((2 * RANGES, 8, 128), F32),
        pltpu.VMEM((D, 128), BF16),
        pltpu.VMEM((WIDE, CHIPS * 128), BF16),
        pltpu.VMEM((WIDE, QKV), BF16),
        pltpu.VMEM((CHIPS - 1, CAP, QKV), BF16),
        pltpu.VMEM((CHIPS - 1, CAP, QKV), BF16),
        pltpu.VMEM((CAP, QKV), F32),
        pltpu.VMEM((256, 128), F32),
        pltpu.VMEM((128, 256), BF16),
        pltpu.VMEM((256, 128), BF16),
        pltpu.VMEM((256, 128), BF16),
        pltpu.VMEM((128, 256), BF16),
        pltpu.VMEM((256, SLOTS * 128), BF16),
        pltpu.VMEM((256, SLOTS * 128), F32),
        pltpu.VMEM((256, SLOTS * 128), F32),
        pltpu.VMEM((256, SLOTS * 128), BF16),
        pltpu.VMEM((256, SLOTS * 128), BF16),
        pltpu.VMEM((256, SLOTS * 128), BF16),
        pltpu.VMEM((256, SLOTS * 128), BF16),
        pltpu.VMEM((QKV, CHIPS * 128), BF16),
        pltpu.VMEM((CHIPS - 1, WIDE, 128), BF16),
        pltpu.VMEM((D, 128), BF16),
        pltpu.VMEM((2, 256, ROWS), BF16),
        pltpu.VMEM((2, 256, ROWS), BF16),
        pltpu.VMEM((2, 256, ROWS), F32),
        pltpu.VMEM((2, 128, ROWS), BF16),
        pltpu.VMEM((2, 128, ROWS), BF16),
        pltpu.VMEM((2, 16, 8, ROWS), F32),
        pltpu.VMEM((2, 16, 8, ROWS), BF16),
        pltpu.VMEM((2, nb - 1, na, 8, ROWS), BF16),
        pltpu.VMEM((2, na, 8, ROWS), F32),
        pltpu.VMEM((2, na, 8, ROWS), BF16),
        pltpu.VMEM((2, na - 1, 1, 8, ROWS), BF16),
        pltpu.VMEM((2, 2, 16, 8, ROWS), BF16),
        dma((6,)),
        dma((RANGES - 1,)), dma((RANGES - 1,)),
        dma, dma,
        dma((CHIPS - 1,)), dma((CHIPS - 1,)),
        dma((CHIPS - 1,)), dma((CHIPS - 1,)),
        dma((REACH,)), dma((REACH,)),
        dma((REACH,)), dma((REACH,)),
        dma((2, CHIPS - 1)), dma((2, CHIPS - 1)),
        dma((CHIPS - 1,)), dma((CHIPS - 1,)),
        dma((2,)), dma((2,)),
        dma((2,)), dma((2,)),
        dma((2, nb - 1)), dma((2, nb - 1)),
        dma((2, na - 1)), dma((2, na - 1)),
        dma((2, na - 1)), dma((2, na - 1)),
        dma((2, nb - 1)), dma((2, nb - 1)),
        dma((2, nb)), dma((2, nb)),
    ]
    d_x, d_wt = pl.pallas_call(
        functools.partial(kernel, zn),
        name="block_backward",
        out_shape=(jax.ShapeDtypeStruct((CAP, D), BF16), jax.ShapeDtypeStruct((QKV, ROWS), F32)),
        in_specs=[pl.BlockSpec(memory_space=pltpu.HBM)] * 6,
        out_specs=(vmem, vmem),
        scratch_shapes=scratch,
        compiler_params=pltpu.CompilerParams(
            collective_id=0, has_side_effects=True, vmem_limit_bytes=50 * 1024 * 1024
        ),
    )(hidden_in, w_qkv, d_attn, range_len, doc_ids, freqs)
    return d_x[None], d_wt.T


def solution(mesh):
    return jax.shard_map(
        functools.partial(body, mesh.shape["dp"] // 2),
        mesh=mesh,
        in_specs=(
            P("dp", "ctx", None),
            P("ctx", None),
            P("dp", "ctx", None),
            P("dp", "ctx"),
            P("dp", "ctx"),
        ),
        out_specs=(P("dp", "ctx", None), P("ctx", None)),
        check_vma=False,
    )
```

time: 149 us -> 142 us (0.953)
  the two profiles are of different devices: /device:TPU:18 before, /device:TPU:2 now
where the time goes in v2:
time: 142 us
  Pallas kernels  134 us (94%)
  local copies, waits for them, and re-layouts  6.74 us (5%)
    pallas_call x1, Pallas kernels, body(): pl.pallas_call(functools.partial(kernel, zn), name='block_backward', out_...  134 us
    unnamed x12, local copies, waits for them, and re-layouts  6.74 us

profile of v2, /device:TPU:2, one launch (start us, length us, event | category | flops | bytes accessed | tf_op | source)
XLA Modules:
  0.0 142.1 jit_solution(2094727506234107272)
XLA Ops:
  1.3 0.0 copy-start
  1.3 1.3 copy-done
  2.6 0.0 copy-start.1
  2.6 1.0 copy-done.1
  3.6 0.0 copy-start.2
  3.6 0.8 copy-done.2
  4.4 0.0 copy-start.3
  4.4 0.8 copy-done.3
  5.2 0.0 copy-start.4
  5.2 0.7 copy-done.4
  5.8 134.1 %block_backward.1 = (bf16[128,5376]{1,0:T(8,128)(2,1)S(1)}, f32[512,336]{1,0:T(8,128)S(1)}) custom-call(bf16[1,128,5376]{2,1,0:T(8,128)(2,1)S(1)} %copy-done, bf16[336,512]{1,0:T(8,128)(2,1)S(1)} %copy-done.1, bf16[1,128,256]{2,1,0:T(8,128)(2,1)S(1)} %copy-done.2, s32[1,1]{1,0:T(1,128)S(6)} %copy.10.len_ref, s32[1,128]{1,0:T(1,128)S(1)} %copy-done.4, ...), custom_call_target="tpu_custom_call" | custom-call | tf_op jit(solution)/shard_map/block_backward/pallas_call | solution.py:531
  139.9 1.1 copy.8
  141.0 1.1 copy.11
Async XLA Ops:
  1.3 1.3 copy-start
  2.6 1.0 copy-start.1
  3.6 0.8 copy-start.2
  4.4 0.8 copy-start.3
  5.2 0.7 copy-start.4
